TPU v7x, 128 devices: a whole 4x4x4 slice. The times are simulated.
128 devices in a mesh: hi: 16 (over y, x), lo: 8 (over z, core).
Axes of the slice: x: 4, y: 4, z: 4, core: 2. Of those that a mesh axis runs over, the one named last changes fastest.
Arguments:
- previous: float32 [32, 2097152], P(None, ('hi', 'lo')), may hold values from -6 to 6
- current: float32 [32, 2097152], P(None, ('hi', 'lo')), may hold values from -6 to 6
- field_levels: int32 [21], replicated, may hold values from -4 to 4
- bond_levels: int32 [20], replicated, may hold values from 1 to 3
Outputs:
- ortho_block: float32 [32, 2097152], P(None, ('hi', 'lo'))
- upper_factor: float32 [32, 32], replicated
All inputs are finite; a program needn't handle non-finite values.
Results may differ from a plain program's by a relative error of at most 0.00005.
Values sent between devices are 32-bit elements; how exact they have to be, the bound alone decides.
A program may use at most 64 MiB of HBM per device.

v0:
```python
import jax
import jax.numpy as jnp
from jax import lax
from jax.sharding import PartitionSpec as P

FIELD_STEP = 0.75
COUPLING_STEP = 0.5


def chain_matrix(couplings, bit_count, bond_list):
    width = 2**bit_count
    rows = lax.iota(jnp.int32, width)[:, None]
    cols = lax.iota(jnp.int32, width)[None, :]
    matrix = jnp.zeros((width, width), jnp.float32)
    for site_number, spot in bond_list:
        differ = cols >> spot & 1 != cols >> spot + 1 & 1
        target = rows == cols ^ 3 << spot
        matrix = matrix + jnp.where(differ & target, 0.5 * couplings[site_number], 0.0)
    return matrix


def cross_flip(values, coupling, low_spot):
    width = values.shape[-1]
    index = lax.iota(jnp.int32, width)
    permute = (index[:, None] == index[None, :] ^ 1 << low_spot).astype(jnp.float32)
    moved = jnp.einsum("vatbl,lj->vatbj", values, permute, precision=lax.Precision.HIGHEST)
    flipped = jnp.flip(moved, axis=2)
    upper = lax.iota(jnp.int32, 2)[:, None]
    keep = (index[None, :] >> low_spot & 1 != upper).astype(jnp.float32)
    return 0.5 * coupling * flipped * keep[None, None, :, None, :]


def local(previous, current, field_levels, bond_levels):
    vectors, amp_count = current.shape
    site_count = field_levels.shape[0]
    devices = lax.axis_size("hi") * lax.axis_size("lo")
    local_bits = amp_count.bit_length() - 1
    global_bits = devices.bit_length() - 1
    rest_bits = local_bits - global_bits
    device = lax.axis_index("hi") * lax.axis_size("lo") + lax.axis_index("lo")
    local_index = lax.iota(jnp.int32, amp_count)
    top_width = 2**global_bits
    low_width = 2**rest_bits

    def position(site_number):
        if site_number < global_bits:
            return rest_bits + site_number
        return site_number - global_bits

    def spin_value(site_number):
        if site_number < local_bits:
            return 0.5 - (local_index >> position(site_number) & 1).astype(jnp.float32)
        return 0.5 - (device >> site_number - local_bits & 1).astype(jnp.float32)

    fields = FIELD_STEP * field_levels.astype(jnp.float32)
    couplings = COUPLING_STEP * bond_levels.astype(jnp.float32)
    diagonal = jnp.zeros((amp_count,), jnp.float32)
    for site_number in range(site_count):
        diagonal = diagonal + fields[site_number] * spin_value(site_number)
        if site_number < site_count - 1:
            diagonal = diagonal + couplings[site_number] * spin_value(site_number) * spin_value(
                site_number + 1
            )
    top_matrix = chain_matrix(
        couplings,
        global_bits,
        [(site_number, site_number) for site_number in range(global_bits - 1)],
    )
    low_matrix = chain_matrix(
        couplings,
        rest_bits,
        [
            (site_number, site_number - global_bits)
            for site_number in range(global_bits, local_bits - 1)
        ],
    )
    blocks = current.reshape(vectors, top_width, low_width)
    applied = diagonal[None, :] * current
    applied = applied + jnp.einsum(
        "vtl,tu->vul", blocks, top_matrix, precision=lax.Precision.HIGHEST
    ).reshape(vectors, amp_count)
    applied = applied + jnp.einsum(
        "vtl,lu->vtu", blocks, low_matrix, precision=lax.Precision.HIGHEST
    ).reshape(vectors, amp_count)
    joined = cross_flip(
        current.reshape(vectors, 1, 2, top_width // 2, low_width), couplings[global_bits - 1], 0
    )
    applied = applied + joined.reshape(vectors, amp_count)
    far_matrix = chain_matrix(
        couplings,
        global_bits,
        [
            (site_number, site_number - local_bits)
            for site_number in range(local_bits, site_count - 1)
        ],
    )
    shaped = current.reshape(vectors, devices, amp_count // devices)
    arrived = lax.all_to_all(shaped, ("hi", "lo"), split_axis=1, concat_axis=1, tiled=True)
    count = arrived.shape[0]
    bond_terms = jnp.einsum(
        "vtl,tu->vul", arrived, far_matrix, precision=lax.Precision.HIGHEST
    ).reshape(count, amp_count)
    seam = cross_flip(
        arrived.reshape(count, top_width // 2, 2, 1, low_width),
        couplings[local_bits - 1],
        rest_bits - 1,
    )
    bond_terms = bond_terms + seam.reshape(count, amp_count)
    remote_part = lax.all_to_all(
        bond_terms.reshape(arrived.shape), ("hi", "lo"), split_axis=1, concat_axis=1, tiled=True
    ).reshape(vectors, amp_count)
    filtered = 4.0 / site_count * (applied + remote_part) - previous
    local_gram = jnp.dot(filtered, filtered.T, precision=lax.Precision.HIGHEST) / (
        amp_count * devices
    )
    gram_matrix = lax.psum(local_gram, ("hi", "lo"))
    lower_factor = jnp.linalg.cholesky(gram_matrix)
    inverse = jax.scipy.linalg.solve_triangular(
        lower_factor, jnp.eye(vectors, dtype=jnp.float32), lower=True
    )
    ortho_block = jnp.dot(inverse, filtered, precision=lax.Precision.HIGHEST)
    return (ortho_block, lower_factor.T)


def solution(mesh):
    in_specs = (P(None, ("hi", "lo")), P(None, ("hi", "lo")), P(), P())
    out_specs = (P(None, ("hi", "lo")), P())
    return jax.shard_map(local, mesh=mesh, in_specs=in_specs, out_specs=out_specs, check_vma=False)
```

profile of v0, /device:TPU:1, one launch (start us, length us, event | category | flops | bytes accessed | tf_op | source)
XLA Modules:
  0.0 200.1 jit_solution(15617030087911046846)
XLA Ops:
  0.6 3.2 %copy_bitcast_fusion = f32[32,128,128]{2,0,1:T(8,128)} fusion(f32[32,16384]{1,0:T(8,128)} %param.5), kind=kLoop, calls=%fused_computation.6 | loop fusion | bytes 4194304 | tf_op jit(solution)/shard_map/reshape | solution.py:77
  3.8 0.0 copy-start
  3.8 0.0 copy-start.1
  3.8 11.5 %all-to-all-start = ((f32[32,128,128]{2,0,1:T(8,128)}), f32[32,128,128]{2,0,1:T(8,128)S(1)}, u32[]{:S(2)}, u32[]{:S(2)}) async-start(f32[32,128,128]{2,0,1:T(8,128)} %copy_bitcast_fusion), calls=%async_computation | async-start | bytes 4194304 | tf_op jit(solution)/shard_map/all_to_all | solution.py:98
  15.3 0.0 copy-done
  15.4 0.7 fusion.153
  20.4 0.0 copy-done.1
  20.4 25.0 %all-to-all-done = f32[32,128,128]{2,0,1:T(8,128)S(1)} async-done(((f32[32,128,128]{2,0,1:T(8,128)}), f32[32,128,128]{2,0,1:T(8,128)S(1)}, u32[]{:S(2)}, u32[]{:S(2)}) %all-to-all-start) | async-done | bytes 2097184 | tf_op jit(solution)/shard_map/all_to_all | solution.py:98
  45.4 2.3 %fusion.7 = f32[32,64,2,128]{3,1,2,0:T(8,128)S(1)} fusion(f32[32,64,2,128]{3,0,2,1:T(8,128)S(1)} %bitcast.129, s32[128]{0:T(128)S(1)} %iota_xor_fusion), kind=kOutput, calls=%fused_computation.14 | convolution fusion | flops 805322752 | bytes 4194816 | tf_op jit(solution)/shard_map/vatbl,lj->vatbj/dot_general | solution.py:26
  47.7 0.3 multiply_multiply_fusion
  48.1 1.7 copy.31
  49.8 3.2 %bitcast_add_fusion.3 = f32[32,128,128]{2,1,0:T(8,128)S(1)} fusion(f32[32,128,128]{2,1,0:T(8,128)S(1)} %bitcast.133, f32[32,128,128]{2,0,1:T(8,128)S(1)} %all-to-all-done, f32[]{:T(128)S(6)} %mul.670, f32[]{:T(128)S(6)} %mul.669, f32[]{:T(128)S(6)} %mul.668, f32[]{:T(128)S(6)} %mul.667, f32[]{:T(128)S(6)} %mul.666, f32[]{:T(128)S(6)} %mul.665, ...), kind=kOutput, calls=%fused_computation.7 | convolution fusion | flops 806207488 | bytes 6295320 | tf_op jit(solution)/shard_map/vtl,tu->vul/dot_general | solution.py:100
  53.0 2.5 %copy.32 = f32[32,128,128]{2,0,1:T(8,128)} copy(f32[32,128,128]{2,1,0:T(8,128)S(1)} %bitcast_add_fusion.3) | data formatting | bytes 4194304 | tf_op jit(solution)/shard_map/add | solution.py:108
  55.5 5.9 %all-to-all-start.1 = ((f32[32,128,128]{2,0,1:T(8,128)}), f32[32,128,128]{2,0,1:T(8,128)}, u32[]{:S(2)}, u32[]{:S(2)}) async-start(f32[32,128,128]{2,0,1:T(8,128)} %copy.32), calls=%async_computation.1 | async-start | bytes 4194304 | tf_op jit(solution)/shard_map/all_to_all | solution.py:109
  61.4 0.7 fusion.151
  74.1 2.0 copy.42
  76.1 3.4 %convolution_bitcast_fusion.1 = f32[32,128,128]{1,2,0:T(8,128)} fusion(f32[32,128,128]{2,1,0:T(8,128)S(1)} %bitcast.125, f32[]{:T(128)S(6)} %mul.659, f32[]{:T(128)S(6)} %mul.658, f32[]{:T(128)S(6)} %mul.657, f32[]{:T(128)S(6)} %mul.656, f32[]{:T(128)S(6)} %mul.655, f32[]{:T(128)S(6)} %mul.654, s32[128]{0:T(128)S(1)} %get-tuple-element.52, ...), kind=kOutput, calls=%fused_computation.16 | convolution fusion | flops 805683200 | bytes 4198168 | tf_op jit(solution)/shard_map/vtl,lu->vtu/dot_general | solution.py:82
  79.5 2.9 %copy.27 = f32[32,128,128]{2,1,0:T(8,128)} copy(f32[32,128,128]{1,2,0:T(8,128)} %convolution_bitcast_fusion.1) | data formatting | bytes 4194304 | tf_op jit(solution)/shard_map/vtl,lu->vtu/dot_general | solution.py:82
  86.2 0.6 fusion.152
  86.7 17.3 %add_add_fusion = f32[16384]{0:T(1024)S(1)} fusion(f32[]{:T(128)S(6)} %mul.645, f32[]{:T(128)S(6)} %mul.644, f32[]{:T(128)S(6)} %mul.642, f32[]{:T(128)S(6)} %mul.641, f32[]{:T(128)S(6)} %mul.639, f32[]{:T(128)S(6)} %mul.638, f32[]{:T(128)S(6)} %mul.636, f32[]{:T(128)S(6)} %mul.635, f32[]{:T(128)S(6)} %mul.633, f32[]{:T(128)S(6)} %mul.632, f32[]{:T(128)S(6)} %mul.630, ...), kind=kLoop, calls=%fused_computation.63 | loop fusion | flops 2260992 | bytes 65704 | tf_op jit(solution)/shard_map/add | solution.py:59
  104.1 1.1 convolution_bitcast_fusion
  105.2 1.6 multiply_multiply_fusion.1
  106.8 3.4 %fusion.14 = f32[128,32,128]{2,0,1:T(8,128)} fusion(f32[32,128,128]{2,1,0:T(8,128)S(1)} %bitcast.127, f32[]{:T(128)S(6)} %mul.653, s32[128]{0:T(128)S(1)} %get-tuple-element.52, f32[]{:T(128)S(6)} %mul.652, s32[128]{0:T(128)S(1)} %get-tuple-element.53, f32[]{:T(128)S(6)} %mul.651, s32[128]{0:T(128)S(1)} %get-tuple-element.54, f32[]{:T(128)S(6)} %mul.650, ...), kind=kOutput, calls=%fused_computation.20 | convolution fusion | flops 805683200 | bytes 4198168 | tf_op jit(solution)/shard_map/vtl,tu->vul/dot_general | solution.py:79
  110.2 0.0 all-to-all-done.1
  110.2 9.6 %fusion.2 = f32[32,16384]{1,0:T(8,128)S(1)} fusion(f32[32,16384]{1,0:T(8,128)} %param.4, f32[4,8,128,128]{3,2,1,0:T(8,128)} %bitcast.130, f32[4,8,128,128]{3,2,1,0:T(8,128)} %bitcast.132, f32[4,8,128,128]{3,2,1,0:T(8,128)} %bitcast.131, f32[32,16384]{1,0:T(8,128)} %param.5, f32[16384]{0:T(1024)S(1)} %add_add_fusion, f32[32,128,128]{2,0,1:T(8,128)} %all-to-all-done.1), kind=kLoop, calls=%fused_computation.3 | loop fusion | flops 3670016 | bytes 14745600 | tf_op jit(solution)/shard_map/sub | solution.py:112
  119.8 1.8 convolution_multiply_fusion
  121.6 67.6 %psum.7 = f32[32,32]{0,1:T(8,128)S(1)} all-reduce(f32[32,32]{0,1:T(8,128)S(1)} %convolution_multiply_fusion), channel_id=1, replica_groups=mesh['hi'=16,'lo'=8] {'hi','lo'}, use_global_device_ids=true, to_apply=%region_0.1 | all-reduce | flops 1024 | bytes 8192 | tf_op jit(solution)/shard_map/psum | solution.py:116
  189.2 0.1 copy.35
  189.3 2.9 %cholesky.17 = f32[32,32]{1,0:T(8,128)S(1)} custom-call(f32[32,32]{1,0:T(8,128)S(1)} %fusion.138), custom_call_target="Cholesky" | custom-call | tf_op jit(solution)/shard_map/jit(cholesky)/cholesky | solution.py:117
  192.2 0.6 compare_reduce_fusion
  192.9 0.7 fusion.139
  193.5 2.4 %custom-call.7 = f32[1,32,32]{1,2,0:T(8,128)S(1)} custom-call(f32[1,32,32]{2,1,0:T(8,128)S(1)} %get-tuple-element.11), custom_call_target="InvertDiagBlocksLowerTriangular" | custom-call | tf_op jit(solution)/shard_map/jit(_solve_triangular)/triangular_solve | solution.py:118
  196.0 0.2 fusion.136
  196.2 3.2 %fusion.154 = f32[32,16384]{1,0:T(8,128)} fusion(f32[32,32]{1,0:T(8,128)S(1)} %fusion.136, f32[32,16384]{1,0:T(8,128)S(1)} %fusion.2), kind=kOutput, calls=%fused_computation.175 | convolution fusion | flops 201326592 | bytes 4198400 | tf_op jit(solution)/shard_map/dot_general | solution.py:121
  199.4 0.7 copy.36
  (16 shorter events, 0.1 us)
Async XLA Ops:
  3.8 11.5 %copy-start = (s32[20]{0:T(128)S(1)}, s32[20]{0:T(128)}, u32[]{:S(2)}) copy-start(s32[20]{0:T(128)} %param.7) | copy-start | bytes 244
  3.8 16.6 %copy-start.1 = (s32[21]{0:T(128)S(1)}, s32[21]{0:T(128)}, u32[]{:S(2)}) copy-start(s32[21]{0:T(128)} %param.6) | copy-start | bytes 256
  3.8 41.6 %all-to-all-start = ((f32[32,128,128]{2,0,1:T(8,128)}), f32[32,128,128]{2,0,1:T(8,128)S(1)}, u32[]{:S(2)}, u32[]{:S(2)}) async-start(f32[32,128,128]{2,0,1:T(8,128)} %copy_bitcast_fusion), calls=%async_computation | async-start | bytes 4194304 | tf_op jit(solution)/shard_map/all_to_all | solution.py:98
  55.5 54.7 %all-to-all-start.1 = ((f32[32,128,128]{2,0,1:T(8,128)}), f32[32,128,128]{2,0,1:T(8,128)}, u32[]{:S(2)}, u32[]{:S(2)}) async-start(f32[32,128,128]{2,0,1:T(8,128)} %copy.32), calls=%async_computation.1 | async-start | bytes 4194304 | tf_op jit(solution)/shard_map/all_to_all | solution.py:109
where the time goes:
time: 201 us; the launch traced here: 200 us
  blocking collectives  67.6 us (34%)
  other arithmetic  35.6 us (18%)
  waiting for transfers between devices  25 us (12%)
  between operations  20.7 us (10%)
  matrix products  18.7 us (9%)
  starting transfers between devices  17.4 us (9%)
  local copies, waits for them, and re-layouts  15.1 us (8%)
    psum x1, blocking collectives, local(): gram_matrix = lax.psum(local_gram, ('hi', 'lo'))  67.6 us
    all_to_all x1, waiting for transfers between devices, local(): lax.all_to_all(shaped, ('hi', 'lo'), split_axis=1, concat_axis=1, tiled=T...  25 us
    add x1, other arithmetic, local(): diagonal = diagonal + fields[site_number] * spin_value(site_number)  17.3 us
    all_to_all x1, starting transfers between devices, local(): lax.all_to_all(shaped, ('hi', 'lo'), split_axis=1, concat_axis=1, tiled=T...  11.5 us
    sub x1, other arithmetic, local(): filtered = 4.0 / site_count * (applied + remote_part) - previous  9.63 us
    all_to_all x1, starting transfers between devices, local(): lax.all_to_all(bond_terms.reshape(arrived.shape), ('hi', 'lo'), split_axi...  5.89 us
  transfers between devices with their start and end apart: 2, of which 1 were waited for; matrix products, arithmetic and copies ran while one was open for 17% of the time, Pallas kernels for 0%

commit v1 on v0

--- a/solution.py
+++ b/solution.py
@@ -113,7 +113,7 @@
     local_gram = jnp.dot(filtered, filtered.T, precision=lax.Precision.HIGHEST) / (
         amp_count * devices
     )
-    gram_matrix = lax.psum(local_gram, ("hi", "lo"))
+    gram_matrix = lax.psum(lax.psum(local_gram, "hi"), axis_name="lo")
     lower_factor = jnp.linalg.cholesky(gram_matrix)
     inverse = jax.scipy.linalg.solve_triangular(
         lower_factor, jnp.eye(vectors, dtype=jnp.float32), lower=True

time: 201 us -> 231 us (1.15)
  blocking collectives: 67.6 us -> 95.5 us
    psum x1 -> x2, blocking collectives: 67.6 us -> 95.5 us  [local(): gram_matrix = lax.psum(lax.psum(local_gram, 'hi'), axis_name='lo')]
  transfers between devices with their start and end apart: 2 -> 2, of which waited for: 1 -> 1; matrix products, arithmetic and copies ran while one was open for 17% -> 15% of each run, Pallas kernels for 0% -> 0%
where the time goes in v1:
time: 231 us; the launch traced here: 228 us
  blocking collectives  95.5 us (41%)
  other arithmetic  35.6 us (15%)
  waiting for transfers between devices  24.8 us (11%)
  between operations  21 us (9%)
  matrix products  18.6 us (8%)
  starting transfers between devices  17.4 us (8%)
  local copies, waits for them, and re-layouts  15.1 us (7%)
    psum x2, blocking collectives, local(): gram_matrix = lax.psum(lax.psum(local_gram, 'hi'), axis_name='lo')  95.5 us
    all_to_all x1, waiting for transfers between devices, local(): lax.all_to_all(shaped, ('hi', 'lo'), split_axis=1, concat_axis=1, tiled=T...  24.8 us
    add x1, other arithmetic, local(): diagonal = diagonal + fields[site_number] * spin_value(site_number)  17.3 us
    all_to_all x1, starting transfers between devices, local(): lax.all_to_all(shaped, ('hi', 'lo'), split_axis=1, concat_axis=1, tiled=T...  11.5 us
    sub x1, other arithmetic, local(): filtered = 4.0 / site_count * (applied + remote_part) - previous  9.63 us
    all_to_all x1, starting transfers between devices, local(): lax.all_to_all(bond_terms.reshape(arrived.shape), ('hi', 'lo'), split_axi...  5.89 us
  transfers between devices with their start and end apart: 2, of which 1 were waited for; matrix products, arithmetic and copies ran while one was open for 15% of the time, Pallas kernels for 0%

profile of v1, /device:TPU:1, one launch (start us, length us, event | category | flops | bytes accessed | tf_op | source)
XLA Modules:
  0.0 228.0 jit_solution(5453678326594752027)
XLA Ops:
  0.6 3.2 %copy_bitcast_fusion = f32[32,128,128]{2,0,1:T(8,128)} fusion(f32[32,16384]{1,0:T(8,128)} %param.5), kind=kLoop, calls=%fused_computation.6 | loop fusion | bytes 4194304 | tf_op jit(solution)/shard_map/reshape | solution.py:77
  3.8 0.0 copy-start
  3.8 0.0 copy-start.1
  3.8 11.5 %all-to-all-start = ((f32[32,128,128]{2,0,1:T(8,128)}), f32[32,128,128]{2,0,1:T(8,128)S(1)}, u32[]{:S(2)}, u32[]{:S(2)}) async-start(f32[32,128,128]{2,0,1:T(8,128)} %copy_bitcast_fusion), calls=%async_computation | async-start | bytes 4194304 | tf_op jit(solution)/shard_map/all_to_all | solution.py:98
  15.3 0.0 copy-done
  15.4 0.7 fusion.153
  20.6 0.0 copy-done.1
  20.7 24.8 %all-to-all-done = f32[32,128,128]{2,0,1:T(8,128)S(1)} async-done(((f32[32,128,128]{2,0,1:T(8,128)}), f32[32,128,128]{2,0,1:T(8,128)S(1)}, u32[]{:S(2)}, u32[]{:S(2)}) %all-to-all-start) | async-done | bytes 2097184 | tf_op jit(solution)/shard_map/all_to_all | solution.py:98
  45.4 2.3 %fusion.7 = f32[32,64,2,128]{3,1,2,0:T(8,128)S(1)} fusion(f32[32,64,2,128]{3,0,2,1:T(8,128)S(1)} %bitcast.129, s32[128]{0:T(128)S(1)} %iota_xor_fusion), kind=kOutput, calls=%fused_computation.14 | convolution fusion | flops 805322752 | bytes 4194816 | tf_op jit(solution)/shard_map/vatbl,lj->vatbj/dot_general | solution.py:26
  47.7 0.3 multiply_multiply_fusion
  48.1 1.7 copy.31
  49.8 3.2 %bitcast_add_fusion.3 = f32[32,128,128]{2,1,0:T(8,128)S(1)} fusion(f32[32,128,128]{2,1,0:T(8,128)S(1)} %bitcast.133, f32[32,128,128]{2,0,1:T(8,128)S(1)} %all-to-all-done, f32[]{:T(128)S(6)} %mul.670, f32[]{:T(128)S(6)} %mul.669, f32[]{:T(128)S(6)} %mul.668, f32[]{:T(128)S(6)} %mul.667, f32[]{:T(128)S(6)} %mul.666, f32[]{:T(128)S(6)} %mul.665, ...), kind=kOutput, calls=%fused_computation.7 | convolution fusion | flops 806207488 | bytes 6295320 | tf_op jit(solution)/shard_map/vtl,tu->vul/dot_general | solution.py:100
  53.0 2.5 %copy.32 = f32[32,128,128]{2,0,1:T(8,128)} copy(f32[32,128,128]{2,1,0:T(8,128)S(1)} %bitcast_add_fusion.3) | data formatting | bytes 4194304 | tf_op jit(solution)/shard_map/add | solution.py:108
  55.5 5.9 %all-to-all-start.1 = ((f32[32,128,128]{2,0,1:T(8,128)}), f32[32,128,128]{2,0,1:T(8,128)}, u32[]{:S(2)}, u32[]{:S(2)}) async-start(f32[32,128,128]{2,0,1:T(8,128)} %copy.32), calls=%async_computation.1 | async-start | bytes 4194304 | tf_op jit(solution)/shard_map/all_to_all | solution.py:109
  61.4 0.7 fusion.151
  74.0 2.0 copy.42
  75.9 3.4 %convolution_bitcast_fusion.1 = f32[32,128,128]{1,2,0:T(8,128)} fusion(f32[32,128,128]{2,1,0:T(8,128)S(1)} %bitcast.125, f32[]{:T(128)S(6)} %mul.659, f32[]{:T(128)S(6)} %mul.658, f32[]{:T(128)S(6)} %mul.657, f32[]{:T(128)S(6)} %mul.656, f32[]{:T(128)S(6)} %mul.655, f32[]{:T(128)S(6)} %mul.654, s32[128]{0:T(128)S(1)} %get-tuple-element.52, ...), kind=kOutput, calls=%fused_computation.16 | convolution fusion | flops 805683200 | bytes 4198168 | tf_op jit(solution)/shard_map/vtl,lu->vtu/dot_general | solution.py:82
  79.4 2.9 %copy.27 = f32[32,128,128]{2,1,0:T(8,128)} copy(f32[32,128,128]{1,2,0:T(8,128)} %convolution_bitcast_fusion.1) | data formatting | bytes 4194304 | tf_op jit(solution)/shard_map/vtl,lu->vtu/dot_general | solution.py:82
  86.1 0.6 fusion.152
  86.7 17.3 %add_add_fusion = f32[16384]{0:T(1024)S(1)} fusion(f32[]{:T(128)S(6)} %mul.645, f32[]{:T(128)S(6)} %mul.644, f32[]{:T(128)S(6)} %mul.642, f32[]{:T(128)S(6)} %mul.641, f32[]{:T(128)S(6)} %mul.639, f32[]{:T(128)S(6)} %mul.638, f32[]{:T(128)S(6)} %mul.636, f32[]{:T(128)S(6)} %mul.635, f32[]{:T(128)S(6)} %mul.633, f32[]{:T(128)S(6)} %mul.632, f32[]{:T(128)S(6)} %mul.630, ...), kind=kLoop, calls=%fused_computation.63 | loop fusion | flops 2260992 | bytes 65704 | tf_op jit(solution)/shard_map/add | solution.py:59
  104.0 1.1 convolution_bitcast_fusion
  105.2 1.6 multiply_multiply_fusion.1
  106.7 3.4 %fusion.14 = f32[128,32,128]{2,0,1:T(8,128)} fusion(f32[32,128,128]{2,1,0:T(8,128)S(1)} %bitcast.127, f32[]{:T(128)S(6)} %mul.653, s32[128]{0:T(128)S(1)} %get-tuple-element.52, f32[]{:T(128)S(6)} %mul.652, s32[128]{0:T(128)S(1)} %get-tuple-element.53, f32[]{:T(128)S(6)} %mul.651, s32[128]{0:T(128)S(1)} %get-tuple-element.54, f32[]{:T(128)S(6)} %mul.650, ...), kind=kOutput, calls=%fused_computation.20 | convolution fusion | flops 805683200 | bytes 4198168 | tf_op jit(solution)/shard_map/vtl,tu->vul/dot_general | solution.py:79
  110.1 0.0 all-to-all-done.1
  110.1 9.6 %fusion.2 = f32[32,16384]{1,0:T(8,128)S(1)} fusion(f32[32,16384]{1,0:T(8,128)} %param.4, f32[4,8,128,128]{3,2,1,0:T(8,128)} %bitcast.130, f32[4,8,128,128]{3,2,1,0:T(8,128)} %bitcast.132, f32[4,8,128,128]{3,2,1,0:T(8,128)} %bitcast.131, f32[32,16384]{1,0:T(8,128)} %param.5, f32[16384]{0:T(1024)S(1)} %add_add_fusion, f32[32,128,128]{2,0,1:T(8,128)} %all-to-all-done.1), kind=kLoop, calls=%fused_computation.3 | loop fusion | flops 3670016 | bytes 14745600 | tf_op jit(solution)/shard_map/sub | solution.py:112
  119.8 1.8 convolution_multiply_fusion
  121.5 60.4 %psum.14 = f32[32,32]{0,1:T(8,128)S(1)} all-reduce(f32[32,32]{0,1:T(8,128)S(1)} %convolution_multiply_fusion), channel_id=1, replica_groups=mesh['hi'=16,'lo'=8] {'hi'}, use_global_device_ids=true, to_apply=%region_0.1 | all-reduce | flops 1024 | bytes 8192 | tf_op jit(solution)/shard_map/psum | solution.py:116
  182.0 35.1 %psum.15 = f32[32,32]{0,1:T(8,128)S(1)} all-reduce(f32[32,32]{0,1:T(8,128)S(1)} %psum.14), channel_id=1, replica_groups=mesh['hi'=16,'lo'=8] {'lo'}, use_global_device_ids=true, to_apply=%region_1.2 | all-reduce | flops 1024 | bytes 8192 | tf_op jit(solution)/shard_map/psum | solution.py:116
  217.1 0.1 copy.35
  217.2 2.9 %cholesky.17 = f32[32,32]{1,0:T(8,128)S(1)} custom-call(f32[32,32]{1,0:T(8,128)S(1)} %fusion.138), custom_call_target="Cholesky" | custom-call | tf_op jit(solution)/shard_map/jit(cholesky)/cholesky | solution.py:117
  220.1 0.6 compare_reduce_fusion
  220.8 0.7 fusion.139
  221.4 2.4 %custom-call.7 = f32[1,32,32]{1,2,0:T(8,128)S(1)} custom-call(f32[1,32,32]{2,1,0:T(8,128)S(1)} %get-tuple-element.11), custom_call_target="InvertDiagBlocksLowerTriangular" | custom-call | tf_op jit(solution)/shard_map/jit(_solve_triangular)/triangular_solve | solution.py:118
  223.8 0.2 fusion.136
  224.1 3.2 %fusion.154 = f32[32,16384]{1,0:T(8,128)} fusion(f32[32,32]{1,0:T(8,128)S(1)} %fusion.136, f32[32,16384]{1,0:T(8,128)S(1)} %fusion.2), kind=kOutput, calls=%fused_computation.175 | convolution fusion | flops 201326592 | bytes 4198400 | tf_op jit(solution)/shard_map/dot_general | solution.py:121
  227.3 0.7 copy.36
  (16 shorter events, 0.1 us)
Async XLA Ops:
  3.8 11.5 %copy-start = (s32[20]{0:T(128)S(1)}, s32[20]{0:T(128)}, u32[]{:S(2)}) copy-start(s32[20]{0:T(128)} %param.7) | copy-start | bytes 244
  3.8 16.8 %copy-start.1 = (s32[21]{0:T(128)S(1)}, s32[21]{0:T(128)}, u32[]{:S(2)}) copy-start(s32[21]{0:T(128)} %param.6) | copy-start | bytes 256
  3.8 41.6 %all-to-all-start = ((f32[32,128,128]{2,0,1:T(8,128)}), f32[32,128,128]{2,0,1:T(8,128)S(1)}, u32[]{:S(2)}, u32[]{:S(2)}) async-start(f32[32,128,128]{2,0,1:T(8,128)} %copy_bitcast_fusion), calls=%async_computation | async-start | bytes 4194304 | tf_op jit(solution)/shard_map/all_to_all | solution.py:98
  55.5 54.7 %all-to-all-start.1 = ((f32[32,128,128]{2,0,1:T(8,128)}), f32[32,128,128]{2,0,1:T(8,128)}, u32[]{:S(2)}, u32[]{:S(2)}) async-start(f32[32,128,128]{2,0,1:T(8,128)} %copy.32), calls=%async_computation.1 | async-start | bytes 4194304 | tf_op jit(solution)/shard_map/all_to_all | solution.py:109
